TPU v7x, 32 devices: a whole 2x2x4 slice. The times are simulated.
32 devices in a mesh: layer: 2 (over x), row: 4 (over z), col: 4 (over y, core).
Axes of the slice: x: 2, y: 2, z: 4, core: 2. Of those that a mesh axis runs over, the one named last changes fastest.
Arguments:
- covariance: float32 [16384, 8192], P(('layer', 'row'), 'col'), parts along dimension 0, may hold values from -2 to 20, as said below
- weight: bfloat16 [16384, 2, 1024], P(('layer', 'col', 'row')), parts along dimension 0, may hold values from -6 to 6
- factor_a: bfloat16 [16384, 2, 256], P(('layer', 'col', 'row')), parts along dimension 0, may hold values from -1.5 to 1.5
- factor_b: bfloat16 [4, 256, 1024], P('layer', ('row', 'col')), parts along dimension 0, may hold values from -1.5 to 1.5
Outputs:
- new_a: float32 [16384, 2, 256], P(('layer', 'col', 'row')), parts along dimension 0
- new_b: float32 [4, 256, 1024], P('layer', ('row', 'col')), parts along dimension 0
There are 2 independent parts, one for each index of `layer`. A program takes and returns all parts, laid end to end along the dimension named above; each array names one. Nothing has to cross between parts.
Inputs may be any that keep to these rules, and one draw needn't show every extreme that they name: covariance is symmetric and positive definite.
All inputs are finite; a program needn't handle non-finite values.
Results may differ from a plain program's by a relative error of at most 0.0012.
Values may be sent and summed in bfloat16 or wider, within the bound.
No kernel may reach another device: no remote copies, remote signals or barrier semaphores. Data moves between devices by JAX's collectives and lax.ppermute only.
A program may use at most 64 MiB of HBM per device.

v0:
```python
import jax
import jax.numpy as jnp
from jax import lax
from jax.sharding import PartitionSpec as P

D = 8192
O = 1024
R = 256


def reorder_slots(spread):
    side = lax.axis_size("row")
    total = side * side
    return spread.reshape(side, side, -1).transpose(1, 0, 2).reshape(total, -1)


def transpose_full(values):
    side = lax.axis_size("row")
    flat = values.reshape(side * side, -1)
    spread = lax.all_to_all(flat, ("row", "col"), split_axis=0, concat_axis=0, tiled=True)
    landed = lax.all_to_all(
        reorder_slots(spread), ("row", "col"), split_axis=0, concat_axis=0, tiled=True
    )
    return landed.reshape(values.shape)


def per_device(covariance, weight, factor_a, factor_b):
    highest = lax.Precision.HIGHEST
    row_count = weight.shape[0]
    full_b = lax.all_gather(factor_b, ("row", "col"), axis=1, tiled=True)
    right_f = full_b.astype(jnp.float32)
    diff_one = (
        weight.astype(jnp.float32)
        - jnp.einsum("nkr,kro->nko", factor_a, full_b, preferred_element_type=jnp.float32)
    ).astype(jnp.bfloat16)
    panels = lax.all_gather(
        jnp.einsum("nko,kro->nkr", diff_one, full_b, preferred_element_type=jnp.float32),
        "row",
        axis=0,
        tiled=True,
    )
    panel_flat = panels.reshape(panels.shape[0], -1)
    cov_rows = covariance
    grad_one = lax.psum_scatter(
        jnp.dot(cov_rows, panel_flat, precision=highest, preferred_element_type=jnp.float32),
        "col",
        scatter_dimension=0,
        tiled=True,
    )
    grad_one = transpose_full(grad_one)
    new_a = factor_a.astype(jnp.float32) + 4.0 / O * grad_one.reshape(row_count, 2, R)
    diff_two = (
        weight.astype(jnp.float32) - jnp.einsum("nkr,kro->nko", new_a, right_f, precision=highest)
    ).astype(jnp.bfloat16)
    a_panel = lax.all_gather(new_a.reshape(row_count, 2 * R), "row", axis=0, tiled=True)
    cov_rows = covariance
    field = lax.psum_scatter(
        jnp.dot(cov_rows, a_panel, precision=highest, preferred_element_type=jnp.float32),
        "col",
        scatter_dimension=0,
        tiled=True,
    )
    field = transpose_full(field)
    partial_value = jnp.einsum(
        "nkr,nko->kro",
        field.reshape(row_count, 2, R),
        diff_two.astype(jnp.float32),
        precision=highest,
    )
    summed = lax.psum(partial_value, ("row", "col"))
    share_rows = factor_b.shape[1]
    linear_id = lax.axis_index("row") * lax.axis_size("col") + lax.axis_index("col")
    own_share = lax.dynamic_slice_in_dim(summed, linear_id * share_rows, share_rows, 1)
    new_b = factor_b.astype(jnp.float32) + 8.0 / D * own_share
    return (new_a, new_b)


def solution(mesh):
    in_specs = (
        P(("layer", "row"), "col"),
        P(("layer", "col", "row"), None, None),
        P(("layer", "col", "row"), None, None),
        P("layer", ("row", "col"), None),
    )
    out_specs = (P(("layer", "col", "row"), None, None), P("layer", ("row", "col"), None))
    return jax.shard_map(
        per_device, mesh=mesh, in_specs=in_specs, out_specs=out_specs, check_vma=False
    )
```

profile of v0, /device:TPU:0, one launch (start us, length us, event | category | flops | bytes accessed | tf_op | source)
XLA Modules:
  0.0 676.0 jit_solution(4953905984134823521)
XLA Ops:
  8.0 4.7 copy.27
  12.7 38.1 %all-gather.4.cloned.1.call-done = bf16[2,256,1024]{2,1,0:T(8,128)(2,1)} async-done(((bf16[2,16,1024]{2,1,0:T(8,128)(2,1)}), bf16[2,256,1024]{2,1,0:T(8,128)(2,1)}) %all-gather.4.cloned.1.call-update) | async-done | bytes 1048592 | tf_op jit(solution)/shard_map/all_gather | solution.py:30
  50.8 4.3 fusion.3
  55.2 79.8 %all-gather.6.cloned.1.call-done = f32[2048,2,256]{2,0,1:T(8,128)} async-done(((f32[512,2,256]{2,0,1:T(8,128)}), f32[2048,2,256]{2,0,1:T(8,128)}) %all-gather.6.cloned.1.call-update) | async-done | bytes 4194320 | tf_op jit(solution)/shard_map/all_gather | solution.py:36
  135.0 5.4 copy.30
  140.4 32.4 %convolution_bitcast_fusion.1 = f32[2048,512]{0,1:T(8,128)} fusion(f32[2048,512]{0,1:T(8,128)} %bitcast.35, f32[2048,2048]{1,0:T(8,128)} %param.4), kind=kOutput, calls=%fused_computation.5 | convolution fusion | flops 25769803776 | bytes 25165824 | tf_op jit(solution)/shard_map/dot_general | solution.py:45
  172.8 43.0 %reduce-scatter.3.cloned.1.call-done = f32[512,512]{0,1:T(8,128)} async-done(((f32[2048,512]{0,1:T(8,128)}), f32[512,512]{0,1:T(8,128)}) %reduce-scatter.3.cloned.1.call-update) | async-done | bytes 1048592 | tf_op jit(solution)/shard_map/reduce_scatter | solution.py:44
  219.6 29.9 %all_to_all.40 = f32[16,1,16384]{2,1,0:T(1,128)S(1)} all-to-all(f32[16,1,16384]{2,1,0:T(1,128)} %all_to_all.32), channel_id=1, replica_groups=mesh['layer'=2,'row'=4,'col'=4] {'row','col'}, dimensions={0} | all-to-all | bytes 2097152 | tf_op jit(solution)/shard_map/all_to_all | solution.py:20
  249.5 3.7 reduce
  259.1 29.5 %all_to_all.41 = f32[16,1,16384]{2,1,0:T(1,128)S(1)} all-to-all(f32[16,1,16384]{2,1,0:T(1,128)S(1)} %all_to_all.33), channel_id=1, replica_groups=mesh['layer'=2,'row'=4,'col'=4] {'row','col'}, dimensions={0} | all-to-all | bytes 2097152 | tf_op jit(solution)/shard_map/all_to_all | solution.py:21
  288.6 3.0 multiply_reduce_fusion
  296.1 81.2 %all-gather.8.cloned.1.call-done = f32[2048,512]{1,0:T(8,128)} async-done(((f32[512,512]{1,0:T(8,128)}), f32[2048,512]{1,0:T(8,128)}) %all-gather.8.cloned.1.call-update) | async-done | bytes 4194320 | tf_op jit(solution)/shard_map/all_gather | solution.py:55
  377.3 57.6 %convolution_bitcast_fusion = f32[2048,512]{0,1:T(8,128)} fusion(f32[2048,512]{1,0:T(8,128)} %all-gather.8.cloned.1.call-done, f32[2048,2048]{1,0:T(8,128)} %param.4), kind=kOutput, calls=%fused_computation.4 | convolution fusion | flops 25769803776 | bytes 25165824 | tf_op jit(solution)/shard_map/dot_general | solution.py:58
  435.0 43.1 %reduce-scatter.5.cloned.1.call-done = f32[512,512]{0,1:T(8,128)} async-done(((f32[2048,512]{0,1:T(8,128)}), f32[512,512]{0,1:T(8,128)}) %reduce-scatter.5.cloned.1.call-update) | async-done | bytes 1048592 | tf_op jit(solution)/shard_map/reduce_scatter | solution.py:57
  480.6 3.4 all_to_all.34
  484.0 29.5 %all_to_all.42 = f32[16,1,16384]{2,1,0:T(1,128)} all-to-all(f32[16,1,16384]{2,1,0:T(1,128)} %all_to_all.34), channel_id=1, replica_groups=mesh['layer'=2,'row'=4,'col'=4] {'row','col'}, dimensions={0} | all-to-all | bytes 2097152 | tf_op jit(solution)/shard_map/all_to_all | solution.py:20
  513.5 4.7 reduce.2
  523.7 3.3 all_to_all.35
  527.0 5.1 all-to-all-start.3
  532.4 4.5 fusion.1
  536.9 18.1 %all-to-all-done.3 = f32[16,1,16384]{2,1,0:T(1,128)} async-done(((f32[16,1,16384]{2,1,0:T(1,128)}), f32[16,1,16384]{2,1,0:T(1,128)}, u32[]{:S(2)}, u32[]{:S(2)}) %all-to-all-start.3) | async-done | bytes 1048608 | tf_op jit(solution)/shard_map/all_to_all | solution.py:21
  555.0 4.7 reduce.3
  561.9 4.8 fusion.4
  566.7 100.4 %all-reduce.2.cloned.1.call-done = f32[2,256,1024]{2,1,0:T(8,128)} async-done(((f32[2,256,1024]{2,1,0:T(8,128)}), f32[2,256,1024]{2,1,0:T(8,128)}) %all-reduce.2.cloned.1.call-update) | async-done | bytes 2097168 | tf_op jit(solution)/shard_map/psum | solution.py:70
  (33 shorter events, 27.0 us)
Async XLA Ops:
  7.2 43.6 %copy-start.2 = (bf16[512,2,256]{2,1,0:T(2,128)(2,1)S(1)}, bf16[512,2,256]{2,1,0:T(2,128)(2,1)}, u32[]{:S(2)}) copy-start(bf16[512,2,256]{2,1,0:T(2,128)(2,1)} %param.6) | copy-start | bytes 1572868
  7.2 43.6 %all-gather.4.cloned.1.call-start = ((), (), s32[]{:S(2)}) async-start(), calls=%async_computation.6 | async-start | bytes 1114112 | tf_op jit(solution)/shard_map/all_gather | solution.py:30
  7.9 127.1 %all-gather.6.cloned.1.call-start = ((), (), s32[]{:S(2)}) async-start(), calls=%async_computation.7 | async-start | bytes 5242880 | tf_op jit(solution)/shard_map/all_gather | solution.py:36
  55.2 160.7 %reduce-scatter.3.cloned.1.call-start = ((), (), s32[]{:S(2)}) async-start(), calls=%async_computation.8 | async-start | bytes 5242880 | tf_op jit(solution)/shard_map/reduce_scatter | solution.py:44
  172.8 204.5 %all-gather.8.cloned.1.call-start = ((), (), s32[]{:S(2)}) async-start(), calls=%async_computation.9 | async-start | bytes 5242880 | tf_op jit(solution)/shard_map/all_gather | solution.py:55
  294.9 237.5 %copy-start = (f32[128,8,256]{2,1,0:T(8,128)}, f32[128,8,256]{2,1,0:T(8,128)S(1)}, u32[]{:S(2)}) copy-start(f32[128,8,256]{2,1,0:T(8,128)S(1)} %convert_add_fusion) | copy-start | bytes 3145732
  296.1 181.9 %reduce-scatter.5.cloned.1.call-start = ((), (), s32[]{:S(2)}) async-start(), calls=%async_computation.10 | async-start | bytes 5242880 | tf_op jit(solution)/shard_map/reduce_scatter | solution.py:57
  527.0 28.0 %all-to-all-start.3 = ((f32[16,1,16384]{2,1,0:T(1,128)}), f32[16,1,16384]{2,1,0:T(1,128)}, u32[]{:S(2)}, u32[]{:S(2)}) async-start(f32[16,1,16384]{2,1,0:T(1,128)} %all_to_all.35), calls=%async_computation.5 | async-start | bytes 2097152 | tf_op jit(solution)/shard_map/all_to_all | solution.py:21
  532.1 135.0 %all-reduce.2.cloned.1.call-start = ((), (), s32[]{:S(2)}) async-start(), calls=%async_computation.11 | async-start | bytes 4194304 | tf_op jit(solution)/shard_map/psum | solution.py:70
  536.9 24.9 %copy-start.1 = (bf16[512,2,1024]{0,2,1:T(8,128)(2,1)S(1)}, bf16[512,2,1024]{0,2,1:T(8,128)(2,1)}, u32[]{:S(2)}) copy-start(bf16[512,2,1024]{0,2,1:T(8,128)(2,1)} %fusion.1) | copy-start | bytes 6291460
  561.9 105.2 %copy-start.3 = (bf16[2,16,1024]{2,1,0:T(8,128)(2,1)S(1)}, bf16[2,16,1024]{2,1,0:T(8,128)(2,1)}, u32[]{:S(2)}) copy-start(bf16[2,16,1024]{2,1,0:T(8,128)(2,1)} %param.7) | copy-start | bytes 196612
Sparse Core Ops, SparseCore 0:
  10.2 40.5 all-gather.3
  55.3 79.7 all-gather.5
  172.9 42.9 reduce-scatter.2
  296.2 81.0 all-gather.7
  435.1 42.9 reduce-scatter.4
  566.8 100.2 all-reduce.1
where the time goes:
time: 683 us; the launch traced here: 676 us
  waiting for transfers between devices  404 us (59%)
  matrix products  104 us (15%)
  blocking collectives  88.9 us (13%)
  local copies, waits for them, and re-layouts  39.6 us (6%)
  other arithmetic  19.2 us (3%)
  between operations  14.7 us (2%)
    psum x1, waiting for transfers between devices, per_device(): summed = lax.psum(partial_value, ('row', 'col'))  100 us
    all_gather x1, waiting for transfers between devices, per_device(): lax.all_gather(new_a.reshape(row_count, 2 * R), 'row', axis=0, tiled=True)  81.2 us
    all_gather x1, waiting for transfers between devices, per_device(): lax.all_gather(jnp.einsum('nko,kro->nkr', diff_one, full_b, preferred_ele...  79.8 us
    all_to_all x2, blocking collectives, transpose_full(): lax.all_to_all(flat, ('row', 'col'), split_axis=0, concat_axis=0, tiled=T...  59.4 us
    dot_general x1, matrix products, per_device(): jnp.dot(cov_rows, a_panel, precision=highest, preferred_element_type=jnp....  57.6 us
    reduce_scatter x1, waiting for transfers between devices, per_device(): lax.psum_scatter(jnp.dot(cov_rows, a_panel, precision=highest, preferred_...  43.1 us
    reduce_scatter x1, waiting for transfers between devices, per_device(): lax.psum_scatter(jnp.dot(cov_rows, panel_flat, precision=highest, preferr...  43 us
    all_gather x1, waiting for transfers between devices, per_device(): full_b = lax.all_gather(factor_b, ('row', 'col'), axis=1, tiled=True)  38.1 us
  transfers between devices with their start and end apart: 7, of which 7 were waited for; matrix products, arithmetic and copies ran while one was open for 1% of the time, Pallas kernels for 0%

commit v1 on v0

--- a/solution.py
+++ b/solution.py
@@ -1,3 +1,4 @@
+import functools
 import jax
 import jax.numpy as jnp
 from jax import lax
@@ -6,6 +7,15 @@
 D = 8192
 O = 1024
 R = 256
+
+
+def lead_ports(frame, ax_name, axis_id):
+    for nth in (ax_name, axis_id):
+        frame = lax.psum(frame, nth)
+    return frame
+
+
+match_the_arrays = functools.partial(lead_ports, ax_name="row", axis_id="col")
 
 
 def reorder_slots(spread):
@@ -67,7 +77,7 @@
         diff_two.astype(jnp.float32),
         precision=highest,
     )
-    summed = lax.psum(partial_value, ("row", "col"))
+    summed = match_the_arrays(partial_value)
     share_rows = factor_b.shape[1]
     linear_id = lax.axis_index("row") * lax.axis_size("col") + lax.axis_index("col")
     own_share = lax.dynamic_slice_in_dim(summed, linear_id * share_rows, share_rows, 1)

time: 683 us -> 724 us (1.060)
  waiting for transfers between devices: 404 us -> 445 us
    psum x1 -> x2, waiting for transfers between devices: 100 us -> 141 us  [lead_ports(): frame = lax.psum(frame, nth)]
  transfers between devices with their start and end apart: 7 -> 8, of which waited for: 7 -> 8; matrix products, arithmetic and copies ran while one was open for 1% -> 1% of each run, Pallas kernels for 0% -> 0%
where the time goes in v1:
time: 724 us; the launch traced here: 717 us
  waiting for transfers between devices  445 us (61%)
  matrix products  104 us (14%)
  blocking collectives  88.9 us (12%)
  local copies, waits for them, and re-layouts  39.6 us (5%)
  other arithmetic  19.2 us (3%)
  between operations  14.7 us (2%)
    psum x2, waiting for transfers between devices, lead_ports(): frame = lax.psum(frame, nth)  141 us
    all_gather x1, waiting for transfers between devices, per_device(): lax.all_gather(new_a.reshape(row_count, 2 * R), 'row', axis=0, tiled=True)  81.2 us
    all_gather x1, waiting for transfers between devices, per_device(): lax.all_gather(jnp.einsum('nko,kro->nkr', diff_one, full_b, preferred_ele...  79.8 us
    all_to_all x2, blocking collectives, transpose_full(): lax.all_to_all(flat, ('row', 'col'), split_axis=0, concat_axis=0, tiled=T...  59.4 us
    dot_general x1, matrix products, per_device(): jnp.dot(cov_rows, a_panel, precision=highest, preferred_element_type=jnp....  57.6 us
    reduce_scatter x1, waiting for transfers between devices, per_device(): lax.psum_scatter(jnp.dot(cov_rows, a_panel, precision=highest, preferred_...  43.1 us
    reduce_scatter x1, waiting for transfers between devices, per_device(): lax.psum_scatter(jnp.dot(cov_rows, panel_flat, precision=highest, preferr...  43 us
    all_gather x1, waiting for transfers between devices, per_device(): full_b = lax.all_gather(factor_b, ('row', 'col'), axis=1, tiled=True)  38.1 us
  transfers between devices with their start and end apart: 8, of which 8 were waited for; matrix products, arithmetic and copies ran while one was open for 1% of the time, Pallas kernels for 0%

profile of v1, /device:TPU:0, one launch (start us, length us, event | category | flops | bytes accessed | tf_op | source)
XLA Modules:
  0.0 716.8 jit_solution(7906713931103597626)
XLA Ops:
  8.0 4.7 copy.27
  12.7 38.1 %all-gather.4.cloned.1.call-done = bf16[2,256,1024]{2,1,0:T(8,128)(2,1)} async-done(((bf16[2,16,1024]{2,1,0:T(8,128)(2,1)}), bf16[2,256,1024]{2,1,0:T(8,128)(2,1)}) %all-gather.4.cloned.1.call-update) | async-done | bytes 1048592 | tf_op jit(solution)/shard_map/all_gather | solution.py:40
  50.8 4.3 fusion.3
  55.2 79.8 %all-gather.6.cloned.1.call-done = f32[2048,2,256]{2,0,1:T(8,128)} async-done(((f32[512,2,256]{2,0,1:T(8,128)}), f32[2048,2,256]{2,0,1:T(8,128)}) %all-gather.6.cloned.1.call-update) | async-done | bytes 4194320 | tf_op jit(solution)/shard_map/all_gather | solution.py:46
  135.0 5.4 copy.30
  140.4 32.4 %convolution_bitcast_fusion.1 = f32[2048,512]{0,1:T(8,128)} fusion(f32[2048,512]{0,1:T(8,128)} %bitcast.35, f32[2048,2048]{1,0:T(8,128)} %param.4), kind=kOutput, calls=%fused_computation.5 | convolution fusion | flops 25769803776 | bytes 25165824 | tf_op jit(solution)/shard_map/dot_general | solution.py:55
  172.8 43.0 %reduce-scatter.3.cloned.1.call-done = f32[512,512]{0,1:T(8,128)} async-done(((f32[2048,512]{0,1:T(8,128)}), f32[512,512]{0,1:T(8,128)}) %reduce-scatter.3.cloned.1.call-update) | async-done | bytes 1048592 | tf_op jit(solution)/shard_map/reduce_scatter | solution.py:54
  219.6 29.9 %all_to_all.40 = f32[16,1,16384]{2,1,0:T(1,128)S(1)} all-to-all(f32[16,1,16384]{2,1,0:T(1,128)} %all_to_all.32), channel_id=1, replica_groups=mesh['layer'=2,'row'=4,'col'=4] {'row','col'}, dimensions={0} | all-to-all | bytes 2097152 | tf_op jit(solution)/shard_map/all_to_all | solution.py:30
  249.5 3.7 reduce
  259.1 29.5 %all_to_all.41 = f32[16,1,16384]{2,1,0:T(1,128)S(1)} all-to-all(f32[16,1,16384]{2,1,0:T(1,128)S(1)} %all_to_all.33), channel_id=1, replica_groups=mesh['layer'=2,'row'=4,'col'=4] {'row','col'}, dimensions={0} | all-to-all | bytes 2097152 | tf_op jit(solution)/shard_map/all_to_all | solution.py:31
  296.1 81.2 %all-gather.8.cloned.1.call-done = f32[2048,512]{1,0:T(8,128)} async-done(((f32[512,512]{1,0:T(8,128)}), f32[2048,512]{1,0:T(8,128)}) %all-gather.8.cloned.1.call-update) | async-done | bytes 4194320 | tf_op jit(solution)/shard_map/all_gather | solution.py:65
  377.3 57.6 %convolution_bitcast_fusion = f32[2048,512]{0,1:T(8,128)} fusion(f32[2048,512]{1,0:T(8,128)} %all-gather.8.cloned.1.call-done, f32[2048,2048]{1,0:T(8,128)} %param.4), kind=kOutput, calls=%fused_computation.4 | convolution fusion | flops 25769803776 | bytes 25165824 | tf_op jit(solution)/shard_map/dot_general | solution.py:68
  435.0 43.1 %reduce-scatter.5.cloned.1.call-done = f32[512,512]{0,1:T(8,128)} async-done(((f32[2048,512]{0,1:T(8,128)}), f32[512,512]{0,1:T(8,128)}) %reduce-scatter.5.cloned.1.call-update) | async-done | bytes 1048592 | tf_op jit(solution)/shard_map/reduce_scatter | solution.py:67
  480.6 3.4 all_to_all.34
  484.0 29.5 %all_to_all.42 = f32[16,1,16384]{2,1,0:T(1,128)} all-to-all(f32[16,1,16384]{2,1,0:T(1,128)} %all_to_all.34), channel_id=1, replica_groups=mesh['layer'=2,'row'=4,'col'=4] {'row','col'}, dimensions={0} | all-to-all | bytes 2097152 | tf_op jit(solution)/shard_map/all_to_all | solution.py:30
  513.5 4.7 reduce.2
  523.7 3.3 all_to_all.35
  527.0 5.1 all-to-all-start.3
  532.4 4.5 fusion.1
  536.9 18.1 %all-to-all-done.3 = f32[16,1,16384]{2,1,0:T(1,128)} async-done(((f32[16,1,16384]{2,1,0:T(1,128)}), f32[16,1,16384]{2,1,0:T(1,128)}, u32[]{:S(2)}, u32[]{:S(2)}) %all-to-all-start.3) | async-done | bytes 1048608 | tf_op jit(solution)/shard_map/all_to_all | solution.py:31
  555.0 4.7 reduce.3
  561.9 4.8 fusion.4
  566.8 88.4 %all-reduce.3.cloned.1.call-done = f32[2,256,1024]{2,1,0:T(8,128)} async-done(((f32[2,256,1024]{2,1,0:T(8,128)}), f32[2,256,1024]{2,1,0:T(8,128)}) %all-reduce.3.cloned.1.call-update) | async-done | bytes 2097168 | tf_op jit(solution)/shard_map/psum | solution.py:14
  655.2 52.8 %all-reduce.5.cloned.1.call-done = f32[2,256,1024]{2,1,0:T(8,128)} async-done(((f32[2,256,1024]{2,1,0:T(8,128)}), f32[2,256,1024]{2,1,0:T(8,128)}) %all-reduce.5.cloned.1.call-update) | async-done | bytes 2097168 | tf_op jit(solution)/shard_map/psum | solution.py:14
  (36 shorter events, 30.0 us)
Async XLA Ops:
  7.2 43.6 %copy-start.2 = (bf16[512,2,256]{2,1,0:T(2,128)(2,1)S(1)}, bf16[512,2,256]{2,1,0:T(2,128)(2,1)}, u32[]{:S(2)}) copy-start(bf16[512,2,256]{2,1,0:T(2,128)(2,1)} %param.6) | copy-start | bytes 1572868
  7.2 43.6 %all-gather.4.cloned.1.call-start = ((), (), s32[]{:S(2)}) async-start(), calls=%async_computation.6 | async-start | bytes 1114112 | tf_op jit(solution)/shard_map/all_gather | solution.py:40
  7.9 127.1 %all-gather.6.cloned.1.call-start = ((), (), s32[]{:S(2)}) async-start(), calls=%async_computation.7 | async-start | bytes 5242880 | tf_op jit(solution)/shard_map/all_gather | solution.py:46
  55.2 160.7 %reduce-scatter.3.cloned.1.call-start = ((), (), s32[]{:S(2)}) async-start(), calls=%async_computation.8 | async-start | bytes 5242880 | tf_op jit(solution)/shard_map/reduce_scatter | solution.py:54
  172.8 204.5 %all-gather.8.cloned.1.call-start = ((), (), s32[]{:S(2)}) async-start(), calls=%async_computation.9 | async-start | bytes 5242880 | tf_op jit(solution)/shard_map/all_gather | solution.py:65
  294.9 237.5 %copy-start = (f32[128,8,256]{2,1,0:T(8,128)}, f32[128,8,256]{2,1,0:T(8,128)S(1)}, u32[]{:S(2)}) copy-start(f32[128,8,256]{2,1,0:T(8,128)S(1)} %convert_add_fusion) | copy-start | bytes 3145732
  296.1 181.9 %reduce-scatter.5.cloned.1.call-start = ((), (), s32[]{:S(2)}) async-start(), calls=%async_computation.10 | async-start | bytes 5242880 | tf_op jit(solution)/shard_map/reduce_scatter | solution.py:67
  527.0 28.0 %all-to-all-start.3 = ((f32[16,1,16384]{2,1,0:T(1,128)}), f32[16,1,16384]{2,1,0:T(1,128)}, u32[]{:S(2)}, u32[]{:S(2)}) async-start(f32[16,1,16384]{2,1,0:T(1,128)} %all_to_all.35), calls=%async_computation.5 | async-start | bytes 2097152 | tf_op jit(solution)/shard_map/all_to_all | solution.py:31
  532.1 123.0 %all-reduce.3.cloned.1.call-start = ((), (), s32[]{:S(2)}) async-start(), calls=%async_computation.11 | async-start | bytes 4194304 | tf_op jit(solution)/shard_map/psum | solution.py:14
  536.9 24.9 %copy-start.1 = (bf16[512,2,1024]{0,2,1:T(8,128)(2,1)S(1)}, bf16[512,2,1024]{0,2,1:T(8,128)(2,1)}, u32[]{:S(2)}) copy-start(bf16[512,2,1024]{0,2,1:T(8,128)(2,1)} %fusion.1) | copy-start | bytes 6291460
  561.9 146.1 %copy-start.3 = (bf16[2,16,1024]{2,1,0:T(8,128)(2,1)S(1)}, bf16[2,16,1024]{2,1,0:T(8,128)(2,1)}, u32[]{:S(2)}) copy-start(bf16[2,16,1024]{2,1,0:T(8,128)(2,1)} %param.7) | copy-start | bytes 196612
  566.7 141.2 %all-reduce.5.cloned.1.call-start = ((), (), s32[]{:S(2)}) async-start(), calls=%async_computation.12 | async-start | bytes 4194304 | tf_op jit(solution)/shard_map/psum | solution.py:14
Sparse Core Ops, SparseCore 0:
  10.2 40.5 all-gather.3
  55.3 79.7 all-gather.5
  172.9 42.9 reduce-scatter.2
  296.2 81.0 all-gather.7
  435.1 42.9 reduce-scatter.4
  566.8 88.2 all-reduce.2
  657.5 50.4 all-reduce.4
